TPU v7x, 128 devices: a whole 4x4x4 slice. The times are simulated.
128 devices in a mesh: rep: 16 (over x_lo, y, core), fsdp: 8 (over x_hi, z).
Axes of the slice: x: 4 (x_hi: 2, x_lo: 2; x = x_hi * 2 + x_lo), y: 4, z: 4, core: 2. Of those that a mesh axis runs over, the one named last changes fastest.
Arguments:
- tokens: bfloat16 [131072, 8192], P(('rep', 'fsdp')), may hold values from -6 to 6
- norm_gain: bfloat16 [8192], replicated, may hold values from 0.25 to 1.75
- deltas: bfloat16 [16, 8192, 1024], P('rep', 'fsdp'), may hold values from -0.09375 to 0.09375
- inner_steps: int32 [16, 16], replicated, may hold values from 1 to 64
- bucket_of_row: int32 [8192], P('fsdp'), may hold values from 0 to 15, never falling along the last dimension, each value on 1 to 1024 neighbouring positions
- master: float32 [8192, 1024], P(('fsdp', 'rep')), may hold values from -0.0625 to 0.0625
- momentum: float32 [8192, 1024], P(('fsdp', 'rep')), may hold values from -0.0625 to 0.0625
Outputs:
- keys: bfloat16 [131072, 1024], P(('rep', 'fsdp'))
- master_new: float32 [8192, 1024], P(('fsdp', 'rep'))
- momentum_new: float32 [8192, 1024], P(('fsdp', 'rep'))
Inputs may be any that keep to these rules, and one draw needn't show every extreme that they name: `bucket_of_row`: never falls along the rows; each bucket holds 1 to 1024 rows.
All inputs are finite; a program needn't handle non-finite values.
Results may differ from a plain program's by a relative error of at most 0.0058.
Values may be sent and summed in bfloat16 or wider, within the bound.
A program may use at most 192 MiB of HBM per device.

v0:
```python
import jax
import jax.numpy as jnp
from jax import lax
from jax.sharding import PartitionSpec as P

OUTER_RATE = 0.7
MOMENTUM_KEEP = 0.9
EPSILON = 1e-05


def normalize(rows, norm_gain):
    values = rows.astype(jnp.float32)
    scale = lax.rsqrt(jnp.mean(values * values, axis=1, keepdims=True) + EPSILON)
    return (values * scale * norm_gain.astype(jnp.float32)[None, :]).astype(jnp.bfloat16)


def on_device(tokens, norm_gain, deltas, inner_steps, bucket_of_row, master, momentum):
    counts = inner_steps.astype(jnp.float32)
    share = counts / jnp.sum(counts, axis=0, keepdims=True)
    own_share = lax.dynamic_slice_in_dim(share, lax.axis_index("rep"), 1, 0)[0]
    bucket_ids = jnp.arange(counts.shape[1], dtype=jnp.int32)
    one_hot = (bucket_of_row[:, None] == bucket_ids[None, :]).astype(jnp.float32)
    row_weight = jnp.sum(one_hot * own_share[None, :], axis=1)
    weighted = row_weight[:, None] * deltas[0].astype(jnp.float32)
    averaged = lax.psum_scatter(weighted, "rep", scatter_dimension=0, tiled=True)
    momentum_new = MOMENTUM_KEEP * momentum + averaged
    master_new = master - OUTER_RATE * (averaged + MOMENTUM_KEEP * momentum_new)
    layer = master_new.astype(jnp.bfloat16)
    normed = normalize(tokens, norm_gain)
    fsdp_count = lax.axis_size("fsdp")
    rep_count = lax.axis_size("rep")
    shard_len = layer.shape[0]
    piece = lax.all_gather(layer, ("rep", "fsdp"), axis=0, tiled=True)
    order = jnp.arange(piece.shape[0], dtype=jnp.int32)
    shard = order // shard_len
    within = order % shard_len
    rep_pos = shard // fsdp_count
    fsdp_pos = shard % fsdp_count
    column_ids = (fsdp_pos * rep_count + rep_pos) * shard_len + within
    columns = jnp.take(normed, column_ids, axis=1)
    projected = jnp.dot(columns, piece, preferred_element_type=jnp.float32)
    return (projected.astype(jnp.bfloat16), master_new, momentum_new)


def solution(mesh):
    in_specs = (
        P(("rep", "fsdp"), None),
        P(),
        P("rep", "fsdp", None),
        P(),
        P("fsdp"),
        P(("fsdp", "rep"), None),
        P(("fsdp", "rep"), None),
    )
    out_specs = (P(("rep", "fsdp"), None), P(("fsdp", "rep"), None), P(("fsdp", "rep"), None))
    return jax.shard_map(
        on_device, mesh=mesh, in_specs=in_specs, out_specs=out_specs, check_vma=False
    )
```

profile of v0, /device:TPU:1, one launch (start us, length us, event | category | flops | bytes accessed | tf_op | source)
XLA Modules:
  0.0 442.1 jit_solution(9010786290908330354)
XLA Ops:
  7.2 0.0 reduce-scatter.2.cloned.1.call-start
  7.2 0.7 convert_element_type.28
  7.9 0.7 convert_reduce_fusion
  8.6 0.8 select_reduce_fusion
  9.4 3.9 convert_multiply_fusion.2
  13.3 0.0 reduce-scatter.2.cloned.1.call-update
  13.3 0.0 all-gather.2.cloned.1.call-start
  13.3 66.3 %reduce-scatter.2.cloned.1.call-done = f32[64,1024]{1,0:T(8,128)} async-done(((f32[1024,1024]{1,0:T(8,128)}), f32[64,1024]{1,0:T(8,128)}) %reduce-scatter.2.cloned.1.call-update) | async-done | bytes 262160 | tf_op jit(solution)/shard_map/reduce_scatter | solution.py:25
  79.7 2.0 fusion.33
  81.7 0.0 all-gather.2.cloned.1.call-update
  81.7 0.0 copy-start.1
  81.7 22.4 %copy.12 = bf16[1024,8192]{0,1:T(8,128)(2,1)} copy(bf16[1024,8192]{1,0:T(8,128)(2,1)} %param.7) | data formatting | bytes 33554432 | tf_op args[0]
  104.2 0.0 copy-done.1
  104.2 0.0 copy-start
  104.2 10.5 %fusion = f32[1024]{0:T(1024)S(1)} fusion(bf16[1024,8192]{0,1:T(8,128)(2,1)} %copy.12), kind=kLoop, calls=%fused_computation.3 | loop fusion | flops 25164800 | bytes 16781312 | tf_op jit(solution)/shard_map/reduce_sum | solution.py:13
  114.7 0.1 compare_select_fusion
  114.8 0.5 copy-done
  115.3 8.0 %fusion.2 = bf16[1024,8192]{0,1:T(8,128)(2,1)} fusion(bf16[1024,8192]{0,1:T(8,128)(2,1)S(1)} %copy-done, f32[8192]{0:T(1024)S(1)} %convert_element_type.26, f32[1024]{0:T(1024)S(1)} %add_rsqrt_fusion), kind=kLoop, calls=%fused_computation.5 | loop fusion | flops 33554432 | bytes 33591296 | tf_op jit(solution)/shard_map/convert_element_type | solution.py:14
  123.3 48.7 %gather_fusion = bf16[8192,1024]{1,0:T(8,128)(2,1)} fusion(bf16[1024,8192]{0,1:T(8,128)(2,1)} %fusion.2, s32[8192]{0:T(1024)S(1)} %broadcast_clamp_fusion), kind=kCustom, calls=%fused_computation | custom fusion | bytes 33587200 | tf_op jit(solution)/shard_map/jit(_take)/gather | solution.py:40
  172.0 239.4 %all-gather.2.cloned.1.call-done = bf16[8192,1024]{1,0:T(8,128)(2,1)} async-done(((bf16[64,1024]{1,0:T(8,128)(2,1)}), bf16[8192,1024]{1,0:T(8,128)(2,1)}) %all-gather.2.cloned.1.call-update) | async-done | bytes 16777232 | tf_op jit(solution)/shard_map/all_gather | solution.py:33
  411.4 23.8 %fusion.7 = bf16[1024,1024]{1,0:T(8,128)(2,1)} fusion(bf16[8192,1024]{1,0:T(8,128)(2,1)} %all-gather.2.cloned.1.call-done, bf16[8192,1024]{1,0:T(8,128)(2,1)} %gather_fusion, pred[8192]{0:T(1024)(128)(4,1)S(1)} %compare_and_fusion), kind=kOutput, calls=%fused_computation.11 | convolution fusion | flops 17189306368 | bytes 35659776 | tf_op jit(solution)/shard_map/dot_general | solution.py:41
  (5 shorter events, 0.1 us)
Async XLA Ops:
  7.2 72.5 %reduce-scatter.2.cloned.1.call-start = ((), (), s32[]{:S(2)}) async-start(), calls=%async_computation.1 | async-start | bytes 4456448 | tf_op jit(solution)/shard_map/reduce_scatter | solution.py:25
  13.3 398.1 %all-gather.2.cloned.1.call-start = ((), (), s32[]{:S(2)}) async-start(), calls=%async_computation.2 | async-start | bytes 16908288 | tf_op jit(solution)/shard_map/all_gather | solution.py:33
  81.7 22.4 %copy-start.1 = (bf16[8192]{0:T(1024)(128)(2,1)S(1)}, bf16[8192]{0:T(1024)(128)(2,1)}, u32[]{:S(2)}) copy-start(bf16[8192]{0:T(1024)(128)(2,1)} %param.8) | copy-start | bytes 49156
  104.2 11.1 %copy-start = (bf16[1024,8192]{0,1:T(8,128)(2,1)S(1)}, bf16[1024,8192]{0,1:T(8,128)(2,1)}, u32[]{:S(2)}) copy-start(bf16[1024,8192]{0,1:T(8,128)(2,1)} %copy.12) | copy-start | bytes 50331652
Sparse Core Ops, SparseCore 0:
  13.4 66.2 reduce-scatter.1
  81.9 329.4 all-gather.1
where the time goes:
time: 443 us; the launch traced here: 442 us
  waiting for transfers between devices  306 us (69%)
  local copies, waits for them, and re-layouts  71.6 us (16%)
  other arithmetic  26.7 us (6%)
  matrix products  23.8 us (5%)
  between operations  14.1 us (3%)
    all_gather x1, waiting for transfers between devices, on_device(): piece = lax.all_gather(layer, ('rep', 'fsdp'), axis=0, tiled=True)  239 us
    reduce_scatter x1, waiting for transfers between devices, on_device(): lax.psum_scatter(weighted, 'rep', scatter_dimension=0, tiled=True)  66.3 us
    gather x1, local copies, waits for them, and re-layouts, on_device(): columns = jnp.take(normed, column_ids, axis=1)  48.7 us
    dot_general x1, matrix products, on_device(): projected = jnp.dot(columns, piece, preferred_element_type=jnp.float32)  23.8 us
    unnamed x5, local copies, waits for them, and re-layouts  22.9 us
    reduce_sum x1, other arithmetic, normalize(): jnp.mean(values * values, axis=1, keepdims=True) + EPSILON  10.5 us
  transfers between devices with their start and end apart: 2, of which 2 were waited for; matrix products, arithmetic and copies ran while one was open for 20% of the time, Pallas kernels for 0%

commit v1 on v0

--- a/solution.py
+++ b/solution.py
@@ -30,7 +30,16 @@
     fsdp_count = lax.axis_size("fsdp")
     rep_count = lax.axis_size("rep")
     shard_len = layer.shape[0]
-    piece = lax.all_gather(layer, ("rep", "fsdp"), axis=0, tiled=True)
+    divide_edges = lambda vals: jnp.concatenate(
+        lax.all_to_all(
+            jnp.stack([vals for _ in range(lax.axis_size(("rep", "fsdp")))], 0),
+            ("rep", "fsdp"),
+            0,
+            0,
+        ),
+        0,
+    )
+    piece = divide_edges(layer)
     order = jnp.arange(piece.shape[0], dtype=jnp.int32)
     shard = order // shard_len
     within = order % shard_len

time: 443 us -> 368 us (0.83)
  waiting for transfers between devices: 306 us -> 215 us
  starting transfers between devices: 0.08 us -> 11 us
  local copies, waits for them, and re-layouts: 71.6 us -> 77.3 us
    all_gather x1 -> x0, waiting for transfers between devices: 239 us -> none  [on_device(): piece = lax.all_gather(layer, ('rep', 'fsdp'), axis=0, tiled=True)]
    all_to_all x0 -> x1, waiting for transfers between devices: none -> 148 us  [on_device(): lax.all_to_all(jnp.stack([vals for _ in range(lax.axis_size(('rep', 'fsdp...]
    all_to_all x0 -> x1, starting transfers between devices: none -> 11 us  [on_device(): lax.all_to_all(jnp.stack([vals for _ in range(lax.axis_size(('rep', 'fsdp...]
    another operation x0 -> x1, local copies, waits for them, and re-layouts: none -> 5.99 us  [on_device(): jnp.stack([vals for _ in range(lax.axis_size(('rep', 'fsdp')))], 0)]
  transfers between devices with their start and end apart: 2 -> 2, of which waited for: 2 -> 2; matrix products, arithmetic and copies ran while one was open for 20% -> 24% of each run, Pallas kernels for 0% -> 0%
where the time goes in v1:
time: 368 us
  waiting for transfers between devices  215 us (58%)
  local copies, waits for them, and re-layouts  77.3 us (21%)
  other arithmetic  26.6 us (7%)
  matrix products  23.8 us (6%)
  between operations  14.1 us (4%)
  starting transfers between devices  11 us (3%)
    all_to_all x1, waiting for transfers between devices, on_device(): lax.all_to_all(jnp.stack([vals for _ in range(lax.axis_size(('rep', 'fsdp...  148 us
    reduce_scatter x1, waiting for transfers between devices, on_device(): lax.psum_scatter(weighted, 'rep', scatter_dimension=0, tiled=True)  66.4 us
    gather x1, local copies, waits for them, and re-layouts, on_device(): columns = jnp.take(normed, column_ids, axis=1)  48.5 us
    dot_general x1, matrix products, on_device(): projected = jnp.dot(columns, piece, preferred_element_type=jnp.float32)  23.8 us
    unnamed x5, local copies, waits for them, and re-layouts  22.7 us
    all_to_all x1, starting transfers between devices, on_device(): lax.all_to_all(jnp.stack([vals for _ in range(lax.axis_size(('rep', 'fsdp...  11 us
    reduce_sum x1, other arithmetic, normalize(): jnp.mean(values * values, axis=1, keepdims=True) + EPSILON  10.5 us
    convert_element_type x1, other arithmetic, normalize(): (values * scale * norm_gain.astype(jnp.float32)[None, :]).astype(jnp.bflo...  7.98 us
  transfers between devices with their start and end apart: 2, of which 2 were waited for; matrix products, arithmetic and copies ran while one was open for 24% of the time, Pallas kernels for 0%

profile of v1, /device:TPU:1, one launch (start us, length us, event | category | flops | bytes accessed | tf_op | source)
XLA Modules:
  0.0 367.6 jit_solution(9912960587243006318)
XLA Ops:
  7.2 0.0 reduce-scatter.2.cloned.1.call-start
  7.2 0.7 convert_element_type.28
  7.9 0.7 convert_reduce_fusion
  8.6 0.8 select_reduce_fusion
  9.4 3.9 %convert_multiply_fusion.2 = f32[1024,1024]{1,0:T(8,128)} fusion(bf16[1,1024,1024]{2,1,0:T(8,128)(2,1)} %param.9, f32[1024]{0:T(1024)S(1)} %select_reduce_fusion), kind=kLoop, calls=%fused_computation.10 | loop fusion | flops 2097152 | bytes 6295552 | tf_op jit(solution)/shard_map/mul | solution.py:24
  13.3 0.0 reduce-scatter.2.cloned.1.call-update
  13.3 66.4 %reduce-scatter.2.cloned.1.call-done = f32[64,1024]{1,0:T(8,128)} async-done(((f32[1024,1024]{1,0:T(8,128)}), f32[64,1024]{1,0:T(8,128)}) %reduce-scatter.2.cloned.1.call-update) | async-done | bytes 262160 | tf_op jit(solution)/shard_map/reduce_scatter | solution.py:25
  79.7 2.0 fusion.33
  81.6 6.0 %stack.2 = bf16[128,64,1024]{2,1,0:T(8,128)(2,1)} broadcast(bf16[64,1024]{1,0:T(8,128)(2,1)S(1)} %get-tuple-element.3), dimensions={1,2} | broadcast | bytes 16908288 | tf_op jit(solution)/shard_map/stack | solution.py:35
  87.6 11.0 %all-to-all-start = ((bf16[128,64,1024]{2,1,0:T(8,128)(2,1)}), bf16[128,64,1024]{2,1,0:T(8,128)(2,1)}, u32[]{:S(2)}, u32[]{:S(2)}) async-start(bf16[128,64,1024]{2,1,0:T(8,128)(2,1)} %stack.2), calls=%async_computation.1 | async-start | bytes 33554432 | tf_op jit(solution)/shard_map/all_to_all | solution.py:34
  98.6 0.0 copy-start.1
  98.6 22.4 %copy.12 = bf16[1024,8192]{0,1:T(8,128)(2,1)} copy(bf16[1024,8192]{1,0:T(8,128)(2,1)} %param.7) | data formatting | bytes 33554432 | tf_op args[0]
  121.1 0.0 copy-done.1
  121.1 0.0 copy-start
  121.1 10.5 %fusion = f32[1024]{0:T(1024)S(1)} fusion(bf16[1024,8192]{0,1:T(8,128)(2,1)} %copy.12), kind=kLoop, calls=%fused_computation.3 | loop fusion | flops 25164800 | bytes 16781312 | tf_op jit(solution)/shard_map/reduce_sum | solution.py:13
  131.6 0.1 compare_select_fusion
  131.7 0.3 copy-done
  132.0 8.0 %fusion.2 = bf16[1024,8192]{0,1:T(8,128)(2,1)} fusion(bf16[1024,8192]{0,1:T(8,128)(2,1)S(1)} %copy-done, f32[8192]{0:T(1024)S(1)} %convert_element_type.26, f32[1024]{0:T(1024)S(1)} %add_rsqrt_fusion), kind=kLoop, calls=%fused_computation.5 | loop fusion | flops 33554432 | bytes 33591296 | tf_op jit(solution)/shard_map/convert_element_type | solution.py:14
  140.0 48.5 %gather_fusion = bf16[8192,1024]{1,0:T(8,128)(2,1)} fusion(bf16[1024,8192]{0,1:T(8,128)(2,1)} %fusion.2, s32[8192]{0:T(1024)S(1)} %broadcast_clamp_fusion), kind=kCustom, calls=%fused_computation | custom fusion | bytes 33587200 | tf_op jit(solution)/shard_map/jit(_take)/gather | solution.py:49
  188.5 148.4 %all-to-all-done = bf16[128,64,1024]{2,1,0:T(8,128)(2,1)} async-done(((bf16[128,64,1024]{2,1,0:T(8,128)(2,1)}), bf16[128,64,1024]{2,1,0:T(8,128)(2,1)}, u32[]{:S(2)}, u32[]{:S(2)}) %all-to-all-start) | async-done | bytes 16777248 | tf_op jit(solution)/shard_map/all_to_all | solution.py:34
  336.9 23.8 %fusion.7 = bf16[1024,1024]{1,0:T(8,128)(2,1)} fusion(bf16[8192,1024]{1,0:T(8,128)(2,1)} %bitcast.3, bf16[8192,1024]{1,0:T(8,128)(2,1)} %gather_fusion, pred[8192]{0:T(1024)(128)(4,1)S(1)} %compare_and_fusion), kind=kOutput, calls=%fused_computation.11 | convolution fusion | flops 17189306368 | bytes 35659776 | tf_op jit(solution)/shard_map/dot_general | solution.py:50
  (5 shorter events, 0.1 us)
Async XLA Ops:
  7.2 72.5 %reduce-scatter.2.cloned.1.call-start = ((), (), s32[]{:S(2)}) async-start(), calls=%async_computation.2 | async-start | bytes 4456448 | tf_op jit(solution)/shard_map/reduce_scatter | solution.py:25
  87.6 249.3 %all-to-all-start = ((bf16[128,64,1024]{2,1,0:T(8,128)(2,1)}), bf16[128,64,1024]{2,1,0:T(8,128)(2,1)}, u32[]{:S(2)}, u32[]{:S(2)}) async-start(bf16[128,64,1024]{2,1,0:T(8,128)(2,1)} %stack.2), calls=%async_computation.1 | async-start | bytes 33554432 | tf_op jit(solution)/shard_map/all_to_all | solution.py:34
  98.6 22.5 %copy-start.1 = (bf16[8192]{0:T(1024)(128)(2,1)S(1)}, bf16[8192]{0:T(1024)(128)(2,1)}, u32[]{:S(2)}) copy-start(bf16[8192]{0:T(1024)(128)(2,1)} %param.8) | copy-start | bytes 49156
  121.1 10.9 %copy-start = (bf16[1024,8192]{0,1:T(8,128)(2,1)S(1)}, bf16[1024,8192]{0,1:T(8,128)(2,1)}, u32[]{:S(2)}) copy-start(bf16[1024,8192]{0,1:T(8,128)(2,1)} %copy.12) | copy-start | bytes 50331652
Sparse Core Ops, SparseCore 0:
  13.4 66.2 reduce-scatter.1
